TPU v7x, 256 devices: a whole 4x4x8 slice. The times are simulated.
256 devices in a mesh: seq: 32 (over y, z), nb: 8 (over x, core).
Axes of the slice: x: 4, y: 4, z: 8, core: 2. Of those that a mesh axis runs over, the one named last changes fastest.
Arguments:
- q_self: bfloat16 [8192, 4096], P('seq', 'nb'), may hold values from -6 to 6
- k_self: bfloat16 [8192, 4096], P('seq', 'nb'), may hold values from -6 to 6
- v_self: bfloat16 [8192, 4096], P('seq', 'nb'), may hold values from -6 to 6
- q_cca: bfloat16 [8192, 4096], P('seq', 'nb'), may hold values from -6 to 6
- memory: bfloat16 [8192, 2, 1024], P('seq'), may hold values from -6 to 6
- database: bfloat16 [65536, 2048], P(('seq', 'nb')), may hold values from -6 to 6
- nbr_block: int32 [2048], P(('seq', 'nb')), may hold values from 0 to 127, as said below
- span_offset: int32 [128], P('seq'), may hold values from 1 to 63
- enc_query: bfloat16 [2048, 1024], P('seq'), may hold values from -0.1355122 to 0.1355122
- enc_out: bfloat16 [1024, 2048], P('seq'), may hold values from -0.1875 to 0.1875
- enc_gain: float32 [2048], replicated, may hold values from 0.5 to 1.5
- cca_kv: bfloat16 [2048, 2, 4096], P(None, None, 'nb'), may hold values from -0.134535646 to 0.134535646
Outputs:
- attended: bfloat16 [8192, 4096], P('seq', 'nb')
Inputs may be any that keep to these rules, and one draw needn't show every extreme that they name: `nbr_block`: block ids are local to a group of 8 devices along nb; the owner of id g is nb index g // 16. Among the 8 requests of one device at most 3 name blocks of one owner, and exactly 3 name blocks of some owner.
All inputs are finite; a program needn't handle non-finite values.
Results may differ from a plain program's by a relative error of at most 0.0041.
Values may be sent and summed in bfloat16 or wider, within the bound.
No kernel may reach another device: no remote copies, remote signals or barrier semaphores. Data moves between devices by JAX's collectives and lax.ppermute only.
A program may use at most 192 MiB of HBM per device.

v0:
```python
import jax
import jax.numpy as jnp
from jax import lax
from jax.sharding import PartitionSpec as P

HD = 128
E = 2048
SPAN = 64
K = 2
R = 128
BLK = 16
masked_score = -1e30


def laid_out(pieces, dim):
    dims = list(pieces.shape[1:])
    dims[dim] *= pieces.shape[0]
    return jnp.moveaxis(pieces, 0, dim).reshape(dims)


def gather_together(arrays, axis, dims):
    ravelled = jnp.concatenate([a.reshape(-1) for a in arrays])
    lines, at, gathered = (lax.all_gather(ravelled, axis), 0, [])
    for a, dim in zip(arrays, dims):
        pieces = lines[:, at : at + a.size].reshape(-1, *a.shape)
        gathered.append(laid_out(pieces, dim))
        at += a.size
    return tuple(gathered)


def passed_along(block, axis, distance):
    devices = range(lax.axis_size(axis))
    route = [(i - distance, i) for i in devices if i - distance in devices]
    return lax.ppermute(block, axis, route)


def local(
    q_self,
    k_self,
    v_self,
    q_cca,
    memory,
    database,
    nbr_block,
    span_offset,
    enc_query,
    enc_out,
    enc_gain,
    cca_kv,
):
    tokens_here = q_self.shape[0]
    head_cols = q_self.shape[1]
    head_count = head_cols // HD
    score_scale = HD ** (-0.5)
    query_start = lax.axis_index("seq") * tokens_here
    query_pos = query_start + jnp.arange(tokens_here, dtype=jnp.int32)
    queries = q_self.reshape(tokens_here, head_count, HD)
    key_part = lax.all_gather(k_self, "seq", axis=0, tiled=True)
    value_part = lax.all_gather(v_self, "seq", axis=0, tiled=True)
    key_count = key_part.shape[0]
    scores = (
        jnp.einsum(
            "qhd,khd->hqk",
            queries,
            key_part.reshape(key_count, head_count, HD),
            preferred_element_type=jnp.float32,
        )
        * score_scale
    )
    key_pos = jnp.arange(key_count, dtype=jnp.int32)
    allowed = (key_pos[None, :] <= query_pos[:, None])[None]
    scores = jnp.where(allowed, scores, masked_score)
    old_max = jnp.full((head_count, tokens_here), masked_score, jnp.float32)
    new_max = jnp.maximum(old_max, jnp.max(scores, axis=2))
    weights_raw = jnp.where(allowed, jnp.exp(scores - new_max[:, :, None]), 0.0)
    new_sum = jnp.sum(weights_raw, axis=2)
    added = jnp.einsum(
        "hqk,khd->hqd",
        weights_raw.astype(jnp.bfloat16),
        value_part.reshape(key_count, head_count, HD),
        preferred_element_type=jnp.float32,
    )
    self_out = (added / new_sum[:, :, None]).transpose(1, 0, 2).reshape(tokens_here, head_cols)
    query_full, output_full = gather_together((enc_query, enc_out), "seq", (0, 0))
    enc_heads = memory.shape[2] // HD
    memory_keys = memory[:, 0].reshape(tokens_here, enc_heads, HD)
    memory_values = memory[:, 1].reshape(tokens_here, enc_heads, HD)
    key_span = jnp.arange(tokens_here, dtype=jnp.int32) // SPAN
    key_open = jnp.arange(tokens_here, dtype=jnp.int32) % SPAN < jnp.repeat(span_offset, SPAN)
    request_count = nbr_block.shape[0]
    owners = lax.axis_size("nb")
    db_count = database.shape[0] // BLK
    capacity = max(2, 3 * request_count // owners)
    owner_ids = nbr_block // db_count
    local_block = nbr_block % db_count
    owner_hits = (owner_ids[:, None] == jnp.arange(owners, dtype=jnp.int32)[None, :]).astype(
        jnp.int32
    )
    rank_within = jnp.sum((jnp.cumsum(owner_hits, axis=0) - 1) * owner_hits, axis=1)
    slot_index = owner_ids * capacity + rank_within
    blocks_span = K * (R // BLK)
    request_place = (
        lax.axis_index("nb") * request_count + jnp.arange(request_count, dtype=jnp.int32) + 1
    )
    request_span = (request_place - 1) // blocks_span
    slot_match = slot_index[None, :] == jnp.arange(owners * capacity, dtype=jnp.int32)[:, None]
    sent_block = jnp.sum(jnp.where(slot_match, local_block[None, :], 0), axis=1)
    sent_span = jnp.sum(jnp.where(slot_match, request_span[None, :], 0), axis=1)
    sent_place = jnp.sum(jnp.where(slot_match, request_place[None, :], 0), axis=1)
    packed = jnp.stack([sent_block, sent_span, sent_place], axis=-1).reshape(owners, capacity, 3)
    db_blocks = database.reshape(db_count, BLK, E)
    request_rows = lax.all_to_all(packed, "nb", split_axis=0, concat_axis=0, tiled=True)
    slot_count = request_rows.shape[1]
    fetched = db_blocks[request_rows[:, :, 0].reshape(-1)].reshape(-1, E)
    exchanged = lax.all_to_all(
        fetched.reshape(owners, slot_count, BLK, E), "nb", split_axis=0, concat_axis=0, tiled=True
    )
    weight_kv = cca_kv.reshape(E, 2 * head_cols)
    own_rows = exchanged.reshape(owners * capacity, BLK, E)[slot_index].reshape(
        request_count * BLK, E
    )
    row_total = own_rows.shape[0]
    wide = own_rows.astype(jnp.float32)
    normed = wide * lax.rsqrt(jnp.mean(wide * wide, axis=1, keepdims=True) + 1e-06) * enc_gain
    enc_q = (
        jnp.dot(normed.astype(jnp.bfloat16), query_full, preferred_element_type=jnp.float32)
        * score_scale
    ).astype(jnp.bfloat16)
    scores = jnp.einsum(
        "nhd,khd->hnk",
        enc_q.reshape(row_total, enc_heads, HD),
        memory_keys,
        preferred_element_type=jnp.float32,
    )
    allowed = ((key_span[None, :] == jnp.repeat(request_span, BLK)[:, None]) & key_open[None, :])[
        None
    ]
    scores = jnp.where(allowed, scores, masked_score)
    row_max = jnp.max(scores, axis=2, keepdims=True)
    weights_raw = jnp.where(allowed, jnp.exp(scores - row_max), 0.0)
    totals = jnp.sum(weights_raw, axis=2)
    context = jnp.einsum(
        "hnk,khd->nhd",
        weights_raw.astype(jnp.bfloat16),
        memory_values,
        preferred_element_type=jnp.float32,
    )
    context = (
        (context / totals.T[:, :, None]).astype(jnp.bfloat16).reshape(row_total, enc_heads * HD)
    )
    own_rows = (wide + jnp.dot(context, output_full, preferred_element_type=jnp.float32)).astype(
        jnp.bfloat16
    )
    group_kv = jnp.dot(
        lax.all_gather(own_rows, "nb", axis=0, tiled=True),
        weight_kv,
        preferred_element_type=jnp.float32,
    ).astype(jnp.bfloat16)
    span_count = span_offset.shape[0]
    group_kv = group_kv.reshape(span_count, K * R, 2 * head_cols)
    before = passed_along(group_kv[-1], "seq", 1)
    stacked = jnp.concatenate([before[None], group_kv], axis=0)
    cross_queries = q_cca.reshape(span_count, SPAN, head_count, HD)

    def attend_block(kv_set):
        key_rows = kv_set[:, :, :head_cols].reshape(span_count, K * R, head_count, HD)
        value_rows = kv_set[:, :, head_cols:].reshape(span_count, K * R, head_count, HD)
        scores = (
            jnp.einsum(
                "ichd,ikhd->ihck", cross_queries, key_rows, preferred_element_type=jnp.float32
            )
            * score_scale
        )
        row_max = jnp.max(scores, axis=3, keepdims=True)
        weights_raw = jnp.exp(scores - row_max)
        totals = jnp.sum(weights_raw, axis=3)
        summed = jnp.einsum(
            "ihck,ikhd->ichd",
            weights_raw.astype(jnp.bfloat16),
            value_rows,
            preferred_element_type=jnp.float32,
        )
        return summed / totals.transpose(0, 2, 1)[:, :, :, None]

    own_part = attend_block(stacked[1:])
    earlier = attend_block(stacked[:-1])
    see_own = (jnp.arange(SPAN, dtype=jnp.int32)[None, :] >= span_offset[:, None])[:, :, None, None]
    cca_out = jnp.where(see_own, own_part, earlier).reshape(tokens_here, head_cols)
    return (self_out + cca_out).astype(jnp.bfloat16)


def solution(mesh):
    in_specs = (
        P("seq", "nb"),
        P("seq", "nb"),
        P("seq", "nb"),
        P("seq", "nb"),
        P("seq", None, None),
        P(("seq", "nb"), None),
        P(("seq", "nb")),
        P("seq"),
        P("seq", None),
        P("seq", None),
        P(),
        P(None, None, "nb"),
    )
    out_specs = P("seq", "nb")
    return jax.shard_map(local, mesh=mesh, in_specs=in_specs, out_specs=out_specs, check_vma=False)
```

profile of v0, /device:TPU:1, one launch (start us, length us, event | category | flops | bytes accessed | tf_op | source)
XLA Modules:
  0.0 394.9 jit_solution(3428079595198629862)
XLA Ops:
  6.5 1.1 copy.92
  7.6 0.9 copy.91
  8.6 0.7 pad_maximum_fusion.2
  9.4 0.7 all-gather.8.cloned.1.call-update
  10.1 0.7 and_select_fusion.4
  10.7 0.1 fusion.45
  10.9 0.2 select_reduce_fusion.3
  11.0 0.1 select_reduce_fusion.2
  11.1 0.1 stack.14
  11.2 0.1 stack.13
  11.3 0.1 stack.12
  11.4 10.2 %all_to_all.10 = s32[8,3,3]{1,2,0:T(4,128)S(1)} all-to-all(s32[8,3,3]{1,2,0:T(4,128)S(1)} %copy.65), channel_id=1, replica_groups=mesh['seq'=32,'nb'=8] {'nb'}, dimensions={0} | all-to-all | bytes 576 | tf_op jit(solution)/shard_map/all_to_all | solution.py:112
  21.7 0.1 reshape_squeeze.9
  21.8 1.8 gather_fusion
  23.6 4.9 %all-to-all-start.1 = ((bf16[8,3,16,2048]{3,2,1,0:T(8,128)(2,1)}), bf16[8,3,16,2048]{3,2,1,0:T(8,128)(2,1)}, u32[]{:S(2)}, u32[]{:S(2)}) async-start(bf16[8,3,16,2048]{3,2,1,0:T(8,128)(2,1)} %bitcast.7), calls=%async_computation.1 | async-start | bytes 3145728 | tf_op jit(solution)/shard_map/all_to_all | solution.py:115
  28.5 1.8 copy.61
  30.4 1.5 fusion.58
  31.9 2.0 copy.69
  33.9 0.9 copy.88
  34.8 0.1 broadcast_in_dim.118
  34.8 0.1 eq.56
  34.9 0.1 ge.18
  35.0 0.1 reshape.313
  35.1 0.1 compare_and_fusion
  35.2 14.0 %all-to-all-done.1 = bf16[8,3,16,2048]{3,2,1,0:T(8,128)(2,1)} async-done(((bf16[8,3,16,2048]{3,2,1,0:T(8,128)(2,1)}), bf16[8,3,16,2048]{3,2,1,0:T(8,128)(2,1)}, u32[]{:S(2)}, u32[]{:S(2)}) %all-to-all-start.1) | async-done | bytes 1572896 | tf_op jit(solution)/shard_map/all_to_all | solution.py:115
  49.2 2.0 gather_fusion.1
  51.2 0.2 multiply_reduce_fusion
  51.4 0.2 multiply_convert_fusion
  51.6 59.4 %all-gather.12.cloned.1.call-done = bf16[4194304]{0:T(1024)(128)(2,1)} async-done(((bf16[131072]{0:T(1024)(128)(2,1)}), bf16[4194304]{0:T(1024)(128)(2,1)}) %all-gather.12.cloned.1.call-update) | async-done | bytes 8388624 | tf_op jit(solution)/shard_map/all_gather | solution.py:23
  111.0 8.7 %reshape.343 = bf16[32,131072]{1,0:T(8,128)(2,1)} reshape(bf16[4194304]{0:T(1024)(128)(2,1)} %all-gather.12.cloned.1.call-done) | data formatting | bytes 16777216 | tf_op jit(solution)/shard_map/all_gather | solution.py:23
  119.7 5.8 %fusion.57 = (bf16[32,65536]{1,0:T(8,128)(2,1)}, bf16[32,65536]{1,0:T(8,128)(2,1)}) fusion(bf16[32,131072]{1,0:T(8,128)(2,1)} %reshape.343), kind=kLoop, calls=%fused_computation.103 | loop fusion | bytes 16777216 | tf_op jit(solution)/shard_map/slice | solution.py:25
  125.5 5.6 %reshape_reshape.10 = bf16[2048,1024]{1,0:T(8,128)(2,1)} reshape(bf16[32,65536]{1,0:T(8,128)(2,1)} %get-tuple-element.11) | data formatting | bytes 8388608 | tf_op jit(solution)/shard_map/reshape;reshape | solution.py:18
  131.2 5.7 %reshape_reshape.11 = bf16[1024,2048]{1,0:T(8,128)(2,1)} reshape(bf16[32,65536]{1,0:T(8,128)(2,1)} %get-tuple-element.10) | data formatting | bytes 8388608 | tf_op jit(solution)/shard_map/reshape;reshape | solution.py:18
  136.9 2.9 fusion.22
  139.8 0.6 fusion.59
  140.4 0.3 convolution_select_fusion
  140.7 0.4 fusion.20
  141.1 3.8 fusion.7
  144.9 5.4 %copy.93 = bf16[256,8,2,512]{3,1,2,0:T(8,128)(2,1)} copy(bf16[256,8,2,512]{3,2,1,0:T(2,128)(2,1)} %bitcast.99) | data formatting | bytes 8388608
  150.3 0.1 reshape.322
  150.4 0.1 iota_compare_fusion.3
  150.4 1.3 iota_compare_fusion
  151.7 56.8 %all-gather.8.cloned.1.call-done = bf16[8192,512]{1,0:T(8,128)(2,1)} async-done(((bf16[256,512]{1,0:T(8,128)(2,1)}), bf16[8192,512]{1,0:T(8,128)(2,1)}) %all-gather.8.cloned.1.call-update) | async-done | bytes 8388624 | tf_op jit(solution)/shard_map/all_gather | solution.py:59
  208.5 11.3 %copy.64 = bf16[8192,512]{0,1:T(8,128)(2,1)} copy(bf16[8192,512]{1,0:T(8,128)(2,1)} %all-gather.8.cloned.1.call-done) | data formatting | bytes 16777216 | tf_op jit(solution)/shard_map/all_gather | solution.py:59
  219.9 88.1 %all-gather.6.cloned.1.call-done = bf16[8192,512]{0,1:T(8,128)(2,1)} async-done(((bf16[256,512]{0,1:T(8,128)(2,1)}), bf16[8192,512]{0,1:T(8,128)(2,1)}) %all-gather.6.cloned.1.call-update) | async-done | bytes 8388624 | tf_op jit(solution)/shard_map/all_gather | solution.py:58
  307.9 18.8 %fusion.1 = (f32[4,256]{1,0:T(4,128)S(1)}, f32[4,256,8192]{2,1,0:T(8,128)}) fusion(pred[256,8192]{1,0:T(8,128)(4,1)S(1)} %iota_compare_fusion, bf16[8192,4,128]{0,2,1:T(8,128)(2,1)} %bitcast.119, bf16[256,512]{1,0:T(8,128)(2,1)S(1)} %copy-done.9), kind=kOutput, calls=%fused_computation.5 | convolution fusion | flops 2172648448 | bytes 44306432 | tf_op jit(solution)/shard_map/qhd,khd->hqk/dot_general | solution.py:62
  326.8 15.9 %fusion.2 = f32[4,256]{1,0:T(4,128)S(1)} fusion(f32[4,256,8192]{2,1,0:T(8,128)} %get-tuple-element.21, f32[4,256]{1,0:T(4,128)S(1)} %broadcast_maximum_fusion, pred[256,8192]{1,0:T(8,128)(4,1)S(1)} %iota_compare_fusion), kind=kLoop, calls=%fused_computation.6 | loop fusion | flops 41942016 | bytes 35659776 | tf_op jit(solution)/shard_map/reduce_sum | solution.py:76
  342.7 4.0 %all-gather.10.cloned.1.call-done = bf16[1024,2048]{1,0:T(8,128)(2,1)} async-done(((bf16[128,2048]{1,0:T(8,128)(2,1)}), bf16[1024,2048]{1,0:T(8,128)(2,1)}) %all-gather.10.cloned.1.call-update) | async-done | bytes 4194320 | tf_op jit(solution)/shard_map/all_gather | solution.py:155
  346.7 7.9 %convolution_convert_fusion = bf16[1024,1024]{1,0:T(8,128)(2,1)S(1)} fusion(bf16[1024,2048]{1,0:T(8,128)(2,1)} %all-gather.10.cloned.1.call-done, bf16[2048,1024]{1,0:T(8,128)(2,1)} %bitcast.100), kind=kOutput, calls=%fused_computation.13 | convolution fusion | flops 4296015872 | bytes 10485760 | tf_op jit(solution)/shard_map/dot_general | solution.py:154
  354.6 1.3 copy-done.3
  356.0 3.2 collective-permute-start
  359.2 17.6 %fusion.23 = f32[256,4,128]{0,2,1:T(8,128)} fusion(bf16[8192,4,128]{0,2,1:T(8,128)(2,1)} %bitcast.95, f32[4,256,8192]{2,1,0:T(8,128)} %get-tuple-element.21, f32[4,256]{1,0:T(4,128)S(1)} %broadcast_maximum_fusion, pred[256,8192]{1,0:T(8,128)(4,1)S(1)} %iota_compare_fusion, f32[256,4]{0,1:T(4,128)S(1)} %bitcast.118), kind=kOutput, calls=%fused_computation.34 | convolution fusion | flops 2189557760 | bytes 44572672 | tf_op jit(solution)/shard_map/hqk,khd->hqd/dot_general | solution.py:77
  376.8 2.0 copy.81
  378.9 2.8 copy.70
  381.7 1.0 copy.75
  382.7 1.6 pad_maximum_fusion
  384.3 0.4 fusion.62
  384.7 0.4 fusion.63
  385.1 0.4 fusion.26
  385.5 0.5 fusion.15
  386.1 0.4 fusion.28
  386.5 0.7 fusion.14
  387.2 0.3 copy.80
  387.6 0.8 fusion.32
  (42 shorter events, 0.3 us)
Async XLA Ops:
  6.5 15.2 %copy-start = (bf16[256,2048]{1,0:T(8,128)(2,1)S(1)}, bf16[256,2048]{1,0:T(8,128)(2,1)}, u32[]{:S(2)}) copy-start(bf16[256,2048]{1,0:T(8,128)(2,1)} %param.17) | copy-start | bytes 3145732
  6.5 23.8 %copy-start.2 = (bf16[256,2,1024]{2,1,0:T(2,128)(2,1)S(1)}, bf16[256,2,1024]{2,1,0:T(2,128)(2,1)}, u32[]{:S(2)}) copy-start(bf16[256,2,1024]{2,1,0:T(2,128)(2,1)} %param.16) | copy-start | bytes 3145732
  6.5 28.4 %copy-start.8 = (s32[4]{0:T(128)S(1)}, s32[4]{0:T(128)}, u32[]{:S(2)}) copy-start(s32[4]{0:T(128)} %param.19) | copy-start | bytes 52
  6.5 104.4 %all-gather.12.cloned.1.call-start = ((), (), s32[]{:S(2)}) async-start(), calls=%async_computation.5 | async-start | bytes 8650752 | tf_op jit(solution)/shard_map/all_gather | solution.py:23
  9.3 42.1 %copy-start.7 = (f32[2048]{0:T(1024)S(1)}, f32[2048]{0:T(1024)}, u32[]{:S(2)}) copy-start(f32[2048]{0:T(1024)} %param.22) | copy-start | bytes 24580
  9.3 199.2 %all-gather.8.cloned.1.call-start = ((), (), s32[]{:S(2)}) async-start(), calls=%async_computation.3 | async-start | bytes 8650752 | tf_op jit(solution)/shard_map/all_gather | solution.py:59
  23.6 25.6 %all-to-all-start.1 = ((bf16[8,3,16,2048]{3,2,1,0:T(8,128)(2,1)}), bf16[8,3,16,2048]{3,2,1,0:T(8,128)(2,1)}, u32[]{:S(2)}, u32[]{:S(2)}) async-start(bf16[8,3,16,2048]{3,2,1,0:T(8,128)(2,1)} %bitcast.7), calls=%async_computation.1 | async-start | bytes 3145728 | tf_op jit(solution)/shard_map/all_to_all | solution.py:115
  28.5 279.4 %all-gather.6.cloned.1.call-start = ((), (), s32[]{:S(2)}) async-start(), calls=%async_computation.2 | async-start | bytes 8650752 | tf_op jit(solution)/shard_map/all_gather | solution.py:58
  30.3 316.3 %all-gather.10.cloned.1.call-start = ((), (), s32[]{:S(2)}) async-start(), calls=%async_computation.4 | async-start | bytes 4718592 | tf_op jit(solution)/shard_map/all_gather | solution.py:155
  131.2 9.5 %copy-start.5 = (bf16[256,1,1024]{0,2,1:T(8,128)(2,1)S(1)}, bf16[256,1,1024]{0,2,1:T(8,128)(2,1)}, u32[]{:S(2)}) copy-start(bf16[256,1,1024]{0,2,1:T(8,128)(2,1)} %copy.69) | copy-start | bytes 1572868
  140.7 9.6 %copy-start.6 = (bf16[256,512]{1,0:T(8,128)(2,1)S(1)}, bf16[256,512]{1,0:T(8,128)(2,1)}, u32[]{:S(2)}) copy-start(bf16[256,512]{1,0:T(8,128)(2,1)} %param.15) | copy-start | bytes 786436
  151.7 156.2 %copy-start.9 = (bf16[256,512]{1,0:T(8,128)(2,1)S(1)}, bf16[256,512]{1,0:T(8,128)(2,1)}, u32[]{:S(2)}) copy-start(bf16[256,512]{1,0:T(8,128)(2,1)} %param.12) | copy-start | bytes 786436
  354.6 1.3 copy-start.3
  356.0 25.7 %collective-permute-start = (bf16[256,1024]{1,0:T(8,128)(2,1)S(1)}, bf16[256,1024]{1,0:T(8,128)(2,1)S(1)}, u32[]{:S(2)}, u32[]{:S(2)}) collective-permute-start(bf16[256,1024]{1,0:T(8,128)(2,1)S(1)} %slice.53), channel_id=1, source_target_pairs={{0,8},{8,16},{16,24},{24,32},{32,40},{40,48},{48,56},{56,64},{64,7... | collective-permute-start | bytes 1572872 | tf_op jit(solution)/shard_map/ppermute | solution.py:34
  382.7 5.6 %copy-start.1 = (bf16[256,2048]{1,0:T(8,128)(2,1)S(1)}, bf16[256,2048]{1,0:T(8,128)(2,1)}, u32[]{:S(2)}) copy-start(bf16[256,2048]{1,0:T(8,128)(2,1)} %param.17) | copy-start | bytes 3145732
  384.3 3.3 copy-start.4
Sparse Core Ops, SparseCore 0:
  9.9 101.0 all-gather.11
  113.6 94.9 all-gather.7
  211.0 96.8 all-gather.5
  309.7 36.9 all-gather.9
where the time goes:
time: 396 us; the launch traced here: 395 us
  waiting for transfers between devices  223 us (56%)
  local copies, waits for them, and re-layouts  62.9 us (16%)
  matrix products  54.5 us (14%)
  other arithmetic  22.7 us (6%)
  between operations  13.4 us (3%)
  blocking collectives  10.2 us (3%)
  starting transfers between devices  8.19 us (2%)
    all_gather x1, waiting for transfers between devices, local(): key_part = lax.all_gather(k_self, 'seq', axis=0, tiled=True)  88.1 us
    all_gather x1, waiting for transfers between devices, gather_together(): lines, at, gathered = (lax.all_gather(ravelled, axis), 0, [])  59.4 us
    all_gather x1, waiting for transfers between devices, local(): value_part = lax.all_gather(v_self, 'seq', axis=0, tiled=True)  56.8 us
    dot_general x1, matrix products, local(): jnp.einsum('qhd,khd->hqk', queries, key_part.reshape(key_count, head_coun...  18.8 us
    dot_general x1, matrix products, local(): jnp.einsum('hqk,khd->hqd', weights_raw.astype(jnp.bfloat16), value_part.r...  17.6 us
    reduce_sum x1, other arithmetic, local(): new_sum = jnp.sum(weights_raw, axis=2)  15.9 us
    all_to_all x1, waiting for transfers between devices, local(): lax.all_to_all(fetched.reshape(owners, slot_count, BLK, E), 'nb', split_a...  14 us
    unnamed x25, local copies, waits for them, and re-layouts  11.4 us
  transfers between devices with their start and end apart: 6, of which 5 were waited for; matrix products, arithmetic and copies ran while one was open for 31% of the time, Pallas kernels for 0%

commit v1 on v0

--- a/solution.py
+++ b/solution.py
@@ -55,7 +55,10 @@
     query_start = lax.axis_index("seq") * tokens_here
     query_pos = query_start + jnp.arange(tokens_here, dtype=jnp.int32)
     queries = q_self.reshape(tokens_here, head_count, HD)
-    key_part = lax.all_gather(k_self, "seq", axis=0, tiled=True)
+    size = lax.axis_size("seq")
+    blocks = jnp.stack([k_self for _ in range(size)])
+    blocks = lax.all_to_all(blocks, "seq", split_axis=0, concat_axis=0)
+    key_part = jnp.concatenate(blocks, axis=0)
     value_part = lax.all_gather(v_self, "seq", axis=0, tiled=True)
     key_count = key_part.shape[0]
     scores = (

time: 396 us -> 452 us (1.14)
  local copies, waits for them, and re-layouts: 62.9 us -> 91.4 us
  waiting for transfers between devices: 223 us -> 239 us
  starting transfers between devices: 8.19 us -> 18.1 us
    all_gather x1 -> x0, waiting for transfers between devices: 88.1 us -> none  [local(): key_part = lax.all_gather(k_self, 'seq', axis=0, tiled=True)]
    all_gather x1, waiting for transfers between devices: 59.4 us -> 136 us  [gather_together(): lines, at, gathered = (lax.all_gather(ravelled, axis), 0, [])]
    all_to_all x0 -> x1, waiting for transfers between devices: none -> 53.8 us  [local(): blocks = lax.all_to_all(blocks, 'seq', split_axis=0, concat_axis=0)]
    all_gather x1, waiting for transfers between devices: 56.8 us -> 34.5 us  [local(): value_part = lax.all_gather(v_self, 'seq', axis=0, tiled=True)]
    another operation x0 -> x2, local copies, waits for them, and re-layouts: none -> 17.7 us  [the longest x1 13.6 us: local(): key_part.reshape(key_count, head_count, HD)]
    all_to_all x0 -> x1, starting transfers between devices: none -> 11.5 us  [local(): blocks = lax.all_to_all(blocks, 'seq', split_axis=0, concat_axis=0)]
    all_to_all x0 -> x1, local copies, waits for them, and re-layouts: none -> 11.4 us  [local(): blocks = lax.all_to_all(blocks, 'seq', split_axis=0, concat_axis=0)]
  transfers between devices with their start and end apart: 6 -> 6, of which waited for: 5 -> 4; matrix products, arithmetic and copies ran while one was open for 31% -> 33% of each run, Pallas kernels for 0% -> 0%
where the time goes in v1:
time: 452 us; the launch traced here: 450 us
  waiting for transfers between devices  239 us (53%)
  local copies, waits for them, and re-layouts  91.4 us (20%)
  matrix products  55 us (12%)
  other arithmetic  22.5 us (5%)
  starting transfers between devices  18.1 us (4%)
  between operations  13.4 us (3%)
  blocking collectives  10.2 us (2%)
    all_gather x1, waiting for transfers between devices, gather_together(): lines, at, gathered = (lax.all_gather(ravelled, axis), 0, [])  136 us
    all_to_all x1, waiting for transfers between devices, local(): blocks = lax.all_to_all(blocks, 'seq', split_axis=0, concat_axis=0)  53.8 us
    all_gather x1, waiting for transfers between devices, local(): value_part = lax.all_gather(v_self, 'seq', axis=0, tiled=True)  34.5 us
    dot_general x1, matrix products, local(): jnp.einsum('qhd,khd->hqk', queries, key_part.reshape(key_count, head_coun...  19.3 us
    dot_general x1, matrix products, local(): jnp.einsum('hqk,khd->hqd', weights_raw.astype(jnp.bfloat16), value_part.r...  17.7 us
    reduce_sum x1, other arithmetic, local(): new_sum = jnp.sum(weights_raw, axis=2)  15.7 us
    all_to_all x1, waiting for transfers between devices, local(): lax.all_to_all(fetched.reshape(owners, slot_count, BLK, E), 'nb', split_a...  14.1 us
    another operation x1, local copies, waits for them, and re-layouts, local(): key_part.reshape(key_count, head_count, HD)  13.6 us
  transfers between devices with their start and end apart: 6, of which 4 were waited for; matrix products, arithmetic and copies ran while one was open for 33% of the time, Pallas kernels for 0%

profile of v1, /device:TPU:1, one launch (start us, length us, event | category | flops | bytes accessed | tf_op | source)
XLA Modules:
  0.0 450.1 jit_solution(2893449387342755766)
XLA Ops:
  6.5 1.1 copy.94
  7.6 0.9 copy.93
  8.6 0.7 pad_maximum_fusion.2
  9.3 0.7 and_select_fusion.4
  10.0 0.1 fusion.45
  10.1 0.2 select_reduce_fusion.3
  10.3 0.1 select_reduce_fusion.2
  10.4 0.1 stack.13
  10.4 0.1 stack.12
  10.5 0.1 stack.11
  10.6 10.2 %all_to_all.15 = s32[8,3,3]{1,2,0:T(4,128)S(1)} all-to-all(s32[8,3,3]{1,2,0:T(4,128)S(1)} %copy.67), channel_id=1, replica_groups=mesh['seq'=32,'nb'=8] {'nb'}, dimensions={0} | all-to-all | bytes 576 | tf_op jit(solution)/shard_map/all_to_all | solution.py:115
  20.9 0.1 reshape_squeeze.9
  21.0 1.9 gather_fusion
  22.9 4.9 %all-to-all-start.2 = ((bf16[8,3,16,2048]{3,2,1,0:T(8,128)(2,1)}), bf16[8,3,16,2048]{3,2,1,0:T(8,128)(2,1)}, u32[]{:S(2)}, u32[]{:S(2)}) async-start(bf16[8,3,16,2048]{3,2,1,0:T(8,128)(2,1)} %bitcast.6), calls=%async_computation.2 | async-start | bytes 3145728 | tf_op jit(solution)/shard_map/all_to_all | solution.py:118
  27.8 0.7 all-gather.5.cloned.1.call-update
  28.6 1.1 copy.62
  29.7 1.5 fusion.58
  31.2 2.0 copy.71
  33.1 0.9 copy.90
  34.1 0.1 eq.56
  34.3 0.1 reshape.311
  34.4 0.1 compare_and_fusion
  34.5 14.1 %all-to-all-done.2 = bf16[8,3,16,2048]{3,2,1,0:T(8,128)(2,1)} async-done(((bf16[8,3,16,2048]{3,2,1,0:T(8,128)(2,1)}), bf16[8,3,16,2048]{3,2,1,0:T(8,128)(2,1)}, u32[]{:S(2)}, u32[]{:S(2)}) %all-to-all-start.2) | async-done | bytes 1572896 | tf_op jit(solution)/shard_map/all_to_all | solution.py:118
  48.5 4.2 stack.10
  52.7 11.5 %all-to-all-start = ((bf16[32,256,512]{1,2,0:T(8,128)(2,1)}), bf16[32,256,512]{1,2,0:T(8,128)(2,1)}, u32[]{:S(2)}, u32[]{:S(2)}) async-start(bf16[32,256,512]{1,2,0:T(8,128)(2,1)} %stack.10), calls=%async_computation | async-start | bytes 16777216 | tf_op jit(solution)/shard_map/all_to_all | solution.py:60
  64.2 2.2 gather_fusion.1
  66.4 0.2 multiply_reduce_fusion
  66.6 0.2 multiply_convert_fusion
  66.8 136.2 %all-gather.9.cloned.1.call-done = bf16[4194304]{0:T(1024)(128)(2,1)} async-done(((bf16[131072]{0:T(1024)(128)(2,1)}), bf16[4194304]{0:T(1024)(128)(2,1)}) %all-gather.9.cloned.1.call-update) | async-done | bytes 8388624 | tf_op jit(solution)/shard_map/all_gather | solution.py:23
  203.1 8.7 %reshape.341 = bf16[32,131072]{1,0:T(8,128)(2,1)} reshape(bf16[4194304]{0:T(1024)(128)(2,1)} %all-gather.9.cloned.1.call-done) | data formatting | bytes 16777216 | tf_op jit(solution)/shard_map/all_gather | solution.py:23
  211.7 5.7 %fusion.57 = (bf16[32,65536]{1,0:T(8,128)(2,1)}, bf16[32,65536]{1,0:T(8,128)(2,1)}) fusion(bf16[32,131072]{1,0:T(8,128)(2,1)} %reshape.341), kind=kLoop, calls=%fused_computation.103 | loop fusion | bytes 16777216 | tf_op jit(solution)/shard_map/slice | solution.py:25
  217.4 5.7 %reshape_reshape.14 = bf16[2048,1024]{1,0:T(8,128)(2,1)} reshape(bf16[32,65536]{1,0:T(8,128)(2,1)} %get-tuple-element.11) | data formatting | bytes 8388608 | tf_op jit(solution)/shard_map/reshape;reshape | solution.py:18
  223.1 5.7 %reshape_reshape.15 = bf16[1024,2048]{1,0:T(8,128)(2,1)} reshape(bf16[32,65536]{1,0:T(8,128)(2,1)} %get-tuple-element.10) | data formatting | bytes 8388608 | tf_op jit(solution)/shard_map/reshape;reshape | solution.py:18
  228.8 2.9 fusion.22
  231.7 0.6 fusion.59
  232.3 0.3 convolution_select_fusion
  232.6 0.4 fusion.20
  233.0 3.9 fusion.7
  236.9 5.3 %copy.95 = bf16[256,8,2,512]{3,1,2,0:T(8,128)(2,1)} copy(bf16[256,8,2,512]{3,2,1,0:T(2,128)(2,1)} %bitcast.100) | data formatting | bytes 8388608
  242.4 0.1 iota_compare_fusion.3
  242.4 1.3 iota_compare_fusion
  243.7 53.8 %all-to-all-done = bf16[32,256,512]{1,2,0:T(8,128)(2,1)} async-done(((bf16[32,256,512]{1,2,0:T(8,128)(2,1)}), bf16[32,256,512]{1,2,0:T(8,128)(2,1)}, u32[]{:S(2)}, u32[]{:S(2)}) %all-to-all-start) | async-done | bytes 8388640 | tf_op jit(solution)/shard_map/all_to_all | solution.py:60
  297.6 11.4 %copy.63 = bf16[32,256,512]{1,0,2:T(8,128)(2,1)} copy(bf16[32,256,512]{1,2,0:T(8,128)(2,1)} %all-to-all-done) | data formatting | bytes 16777216 | tf_op jit(solution)/shard_map/all_to_all | solution.py:60
  308.9 13.6 %reshape_reshape.12 = bf16[8192,4,128]{0,2,1:T(8,128)(2,1)} reshape(bf16[32,256,512]{1,0,2:T(8,128)(2,1)} %copy.63) | data formatting | bytes 16777216 | tf_op jit(solution)/shard_map/reshape;reshape | solution.py:68
  322.5 34.5 %all-gather.5.cloned.1.call-done = bf16[8192,512]{1,0:T(8,128)(2,1)} async-done(((bf16[256,512]{1,0:T(8,128)(2,1)}), bf16[8192,512]{1,0:T(8,128)(2,1)}) %all-gather.5.cloned.1.call-update) | async-done | bytes 8388624 | tf_op jit(solution)/shard_map/all_gather | solution.py:62
  357.0 11.3 %copy.66 = bf16[8192,512]{0,1:T(8,128)(2,1)} copy(bf16[8192,512]{1,0:T(8,128)(2,1)} %all-gather.5.cloned.1.call-done) | data formatting | bytes 16777216 | tf_op jit(solution)/shard_map/all_gather | solution.py:62
  368.3 19.3 %fusion.1 = (f32[4,256]{1,0:T(4,128)S(1)}, f32[4,256,8192]{2,1,0:T(8,128)}) fusion(pred[256,8192]{1,0:T(8,128)(4,1)S(1)} %iota_compare_fusion, bf16[8192,4,128]{0,2,1:T(8,128)(2,1)} %reshape_reshape.12, bf16[256,512]{1,0:T(8,128)(2,1)S(1)} %copy-done.9), kind=kOutput, calls=%fused_computation.5 | convolution fusion | flops 2172648448 | bytes 44306432 | tf_op jit(solution)/shard_map/qhd,khd->hqk/dot_general | solution.py:65
  387.6 15.7 %fusion.2 = f32[4,256]{1,0:T(4,128)S(1)} fusion(f32[4,256,8192]{2,1,0:T(8,128)} %get-tuple-element.21, f32[4,256]{1,0:T(4,128)S(1)} %broadcast_maximum_fusion, pred[256,8192]{1,0:T(8,128)(4,1)S(1)} %iota_compare_fusion), kind=kLoop, calls=%fused_computation.6 | loop fusion | flops 41942016 | bytes 35659776 | tf_op jit(solution)/shard_map/reduce_sum | solution.py:79
  403.3 8.0 %convolution_convert_fusion = bf16[1024,1024]{1,0:T(8,128)(2,1)S(1)} fusion(bf16[1024,2048]{1,0:T(8,128)(2,1)} %all-gather.7.cloned.1.call-done, bf16[2048,1024]{1,0:T(8,128)(2,1)} %bitcast.101), kind=kOutput, calls=%fused_computation.13 | convolution fusion | flops 4296015872 | bytes 10485760 | tf_op jit(solution)/shard_map/dot_general | solution.py:157
  411.3 1.3 copy-done.3
  412.6 1.7 collective-permute-start
  414.4 17.7 %fusion.23 = f32[256,4,128]{0,2,1:T(8,128)} fusion(bf16[8192,4,128]{0,2,1:T(8,128)(2,1)} %bitcast.96, f32[4,256,8192]{2,1,0:T(8,128)} %get-tuple-element.21, f32[4,256]{1,0:T(4,128)S(1)} %broadcast_maximum_fusion, pred[256,8192]{1,0:T(8,128)(4,1)S(1)} %iota_compare_fusion, f32[256,4]{0,1:T(4,128)S(1)} %bitcast.119), kind=kOutput, calls=%fused_computation.34 | convolution fusion | flops 2189557760 | bytes 44572672 | tf_op jit(solution)/shard_map/hqk,khd->hqd/dot_general | solution.py:80
  432.1 2.0 copy.83
  434.1 2.8 copy.72
  437.0 1.0 copy.77
  438.0 1.6 pad_maximum_fusion
  439.6 0.4 fusion.62
  440.0 0.4 fusion.63
  440.4 0.4 fusion.26
  440.8 0.5 fusion.15
  441.3 0.4 fusion.28
  441.7 0.7 fusion.14
  442.5 0.3 copy.82
  442.8 0.8 fusion.32
  (44 shorter events, 0.5 us)
Async XLA Ops:
  6.5 14.4 %copy-start = (bf16[256,2048]{1,0:T(8,128)(2,1)S(1)}, bf16[256,2048]{1,0:T(8,128)(2,1)}, u32[]{:S(2)}) copy-start(bf16[256,2048]{1,0:T(8,128)(2,1)} %param.17) | copy-start | bytes 3145732
  6.5 23.1 %copy-start.2 = (bf16[256,2,1024]{2,1,0:T(2,128)(2,1)S(1)}, bf16[256,2,1024]{2,1,0:T(2,128)(2,1)}, u32[]{:S(2)}) copy-start(bf16[256,2,1024]{2,1,0:T(2,128)(2,1)} %param.16) | copy-start | bytes 3145732
  6.5 27.7 %copy-start.8 = (s32[4]{0:T(128)S(1)}, s32[4]{0:T(128)}, u32[]{:S(2)}) copy-start(s32[4]{0:T(128)} %param.19) | copy-start | bytes 52
  6.5 196.5 %all-gather.9.cloned.1.call-start = ((), (), s32[]{:S(2)}) async-start(), calls=%async_computation.5 | async-start | bytes 8650752 | tf_op jit(solution)/shard_map/all_gather | solution.py:23
  22.9 25.6 %all-to-all-start.2 = ((bf16[8,3,16,2048]{3,2,1,0:T(8,128)(2,1)}), bf16[8,3,16,2048]{3,2,1,0:T(8,128)(2,1)}, u32[]{:S(2)}, u32[]{:S(2)}) async-start(bf16[8,3,16,2048]{3,2,1,0:T(8,128)(2,1)} %bitcast.6), calls=%async_computation.2 | async-start | bytes 3145728 | tf_op jit(solution)/shard_map/all_to_all | solution.py:118
  27.8 329.2 %all-gather.5.cloned.1.call-start = ((), (), s32[]{:S(2)}) async-start(), calls=%async_computation.3 | async-start | bytes 8650752 | tf_op jit(solution)/shard_map/all_gather | solution.py:62
  52.7 13.9 %copy-start.7 = (f32[2048]{0:T(1024)S(1)}, f32[2048]{0:T(1024)}, u32[]{:S(2)}) copy-start(f32[2048]{0:T(1024)} %param.22) | copy-start | bytes 24580
  52.7 244.8 %all-to-all-start = ((bf16[32,256,512]{1,2,0:T(8,128)(2,1)}), bf16[32,256,512]{1,2,0:T(8,128)(2,1)}, u32[]{:S(2)}, u32[]{:S(2)}) async-start(bf16[32,256,512]{1,2,0:T(8,128)(2,1)} %stack.10), calls=%async_computation | async-start | bytes 16777216 | tf_op jit(solution)/shard_map/all_to_all | solution.py:60
  64.2 339.1 %all-gather.7.cloned.1.call-start = ((), (), s32[]{:S(2)}) async-start(), calls=%async_computation.4 | async-start | bytes 4718592 | tf_op jit(solution)/shard_map/all_gather | solution.py:158
  223.1 9.5 %copy-start.5 = (bf16[256,1,1024]{0,2,1:T(8,128)(2,1)S(1)}, bf16[256,1,1024]{0,2,1:T(8,128)(2,1)}, u32[]{:S(2)}) copy-start(bf16[256,1,1024]{0,2,1:T(8,128)(2,1)} %copy.71) | copy-start | bytes 1572868
  232.6 9.7 %copy-start.6 = (bf16[256,512]{1,0:T(8,128)(2,1)S(1)}, bf16[256,512]{1,0:T(8,128)(2,1)}, u32[]{:S(2)}) copy-start(bf16[256,512]{1,0:T(8,128)(2,1)} %param.15) | copy-start | bytes 786436
  322.5 45.8 %copy-start.9 = (bf16[256,512]{1,0:T(8,128)(2,1)S(1)}, bf16[256,512]{1,0:T(8,128)(2,1)}, u32[]{:S(2)}) copy-start(bf16[256,512]{1,0:T(8,128)(2,1)} %param.12) | copy-start | bytes 786436
  411.3 1.4 copy-start.3
  412.6 24.3 %collective-permute-start = (bf16[256,1024]{1,0:T(8,128)(2,1)S(1)}, bf16[256,1024]{1,0:T(8,128)(2,1)S(1)}, u32[]{:S(2)}, u32[]{:S(2)}) collective-permute-start(bf16[256,1024]{1,0:T(8,128)(2,1)S(1)} %slice.53), channel_id=1, source_target_pairs={{0,8},{8,16},{16,24},{24,32},{32,40},{40,48},{48,56},{56,64},{64,7... | collective-permute-start | bytes 1572872 | tf_op jit(solution)/shard_map/ppermute | solution.py:34
  438.0 5.6 %copy-start.1 = (bf16[256,2048]{1,0:T(8,128)(2,1)S(1)}, bf16[256,2048]{1,0:T(8,128)(2,1)}, u32[]{:S(2)}) copy-start(bf16[256,2048]{1,0:T(8,128)(2,1)} %param.17) | copy-start | bytes 3145732
  439.6 3.3 copy-start.4
Sparse Core Ops, SparseCore 0:
  9.9 193.0 all-gather.8
  205.7 151.2 all-gather.4
  358.9 32.7 all-gather.6
